TPU v7x, 32 devices: a whole 2x2x4 slice. The times are simulated.
32 devices in a mesh: dom: 8 (over z, y), tm: 4 (over x, core).
Axes of the slice: x: 2, y: 2, z: 4, core: 2. Of those that a mesh axis runs over, the one named last changes fastest.
Arguments:
- panel_signal: bfloat16 [8, 8192], P('tm', 'dom'), may hold values from -6 to 6
- panel_box: int32 [8192], P('dom'), may hold values from 0 to 15
- radiation: bfloat16 [8192, 1024], P('dom'), may hold values from -0.75 to 0.75
- reception: bfloat16 [8192, 1024], P('dom'), may hold values from -0.1875 to 0.1875
- translation: bfloat16 [64, 8, 1024], P(None, None, 'dom'), may hold values from -1 to 1
- list_source: int32 [128, 8], replicated, may hold values from 0 to 127
- list_class: int32 [128, 8], replicated, may hold values from 0 to 63
- list_count: int32 [128], replicated, may hold values from 1 to 8, as said below
Outputs:
- panel_field: bfloat16 [8, 8192], P('tm', 'dom')
Inputs may be any that keep to these rules, and one draw needn't show every extreme that they name: `panel_box`: indices a panel's box among the 16 boxes of its own index of dom. Box a uses the first list_count[a] entries of its lists; the rest are padding.
All inputs are finite; a program needn't handle non-finite values.
Results may differ from a plain program's by a relative error of at most 0.0057.
Values may be sent and summed in bfloat16 or wider, within the bound.
A program may use at most 64 MiB of HBM per device.

v0:
```python
import math
import jax
import jax.numpy as jnp
from jax import lax
from jax.sharding import PartitionSpec as P

BOX_DEV = 16
J = 8


def lag_sum(kern_rows, gathered, out_steps, offset):
    entries = kern_rows.shape[0]
    lags_all = kern_rows.shape[1]
    width = kern_rows.shape[2]
    results = []
    for step_out in range(out_steps):
        total = jnp.zeros((entries, width), jnp.float32)
        for step_in in range(gathered.shape[1]):
            delay = offset + step_out - step_in
            picked = lax.dynamic_index_in_dim(
                kern_rows, jnp.clip(delay, 0, lags_all - 1), 1, keepdims=False
            )
            weight = jnp.where(delay >= 0, picked.astype(jnp.float32), 0.0)
            total = total + weight * gathered[:, step_in].astype(jnp.float32)
        results.append(total)
    return jnp.stack(results, axis=1)


def body(
    panel_signal, panel_box, radiation, reception, translation, list_source, list_class, list_count
):
    rows_own = panel_signal.shape[0]
    dirs_own = translation.shape[2]
    boxes_all = list_source.shape[0]
    classes_all = translation.shape[0]
    lags_all = translation.shape[1]
    box_onehot = (panel_box[None, :] == jnp.arange(BOX_DEV, dtype=jnp.int32)[:, None]).astype(
        jnp.bfloat16
    )
    used_rows = (jnp.arange(J, dtype=jnp.int32)[None, :] < list_count[:, None]).astype(jnp.bfloat16)
    block_size = math.gcd(boxes_all, 256)

    def translate_all(table, rays, out_steps, offset):
        width = table.shape[2]
        count_in = rays.shape[1]
        flat_table = table.reshape(classes_all, lags_all * width)
        flat_rays = rays.reshape(boxes_all, count_in * width)

        def one_block(index):
            sources = lax.dynamic_slice_in_dim(
                list_source, index * block_size, block_size, 0
            ).reshape(block_size * J)
            classes = lax.dynamic_slice_in_dim(
                list_class, index * block_size, block_size, 0
            ).reshape(block_size * J)
            keep_rows = lax.dynamic_slice_in_dim(
                used_rows, index * block_size, block_size, 0
            ).reshape(block_size * J, 1)
            kern_rows = (jnp.take(flat_table, classes, axis=0) * keep_rows).reshape(
                block_size * J, lags_all, width
            )
            gathered = jnp.take(flat_rays, sources, axis=0).reshape(block_size * J, count_in, width)
            summed = lag_sum(kern_rows, gathered, out_steps, offset)
            return jnp.sum(summed.reshape(block_size, J, out_steps, width), axis=1)

        blocks = lax.map(one_block, jnp.arange(boxes_all // block_size, dtype=jnp.int32))
        return blocks.reshape(boxes_all, out_steps, width)

    masked = panel_signal[:, None, :] * box_onehot[None]
    outgoing = jnp.einsum(
        "rbp,pk->brk", masked, radiation, preferred_element_type=jnp.float32
    ).astype(jnp.bfloat16)
    spread = lax.all_to_all(outgoing, "dom", split_axis=2, concat_axis=0, tiled=True)
    first = lax.axis_index("tm") * rows_own
    empty = jnp.zeros((boxes_all, rows_own, dirs_own), jnp.float32)
    piece = lax.all_gather(spread, "tm", axis=1, tiled=True)

    def active():
        return empty + translate_all(translation, piece, rows_own, first)

    def passive():
        return empty

    incoming = lax.cond(jnp.int32(0) <= first + rows_own - 1, active, passive)
    rays = lax.all_to_all(
        incoming.astype(jnp.bfloat16), "dom", split_axis=0, concat_axis=2, tiled=True
    )
    partial_value = jnp.einsum("brk,pk->brp", rays, reception, preferred_element_type=jnp.float32)
    field = jnp.sum(partial_value * box_onehot.astype(jnp.float32)[:, None, :], axis=0)
    return field.astype(jnp.bfloat16)


def solution(mesh):
    placed = (
        P("tm", "dom"),
        P("dom"),
        P("dom", None),
        P("dom", None),
        P(None, None, "dom"),
        P(),
        P(),
        P(),
    )
    return jax.shard_map(
        body, mesh=mesh, in_specs=placed, out_specs=P("tm", "dom"), check_vma=False
    )
```

profile of v0, /device:TPU:0, one launch (start us, length us, event | category | flops | bytes accessed | tf_op | source)
XLA Modules:
  0.0 77.4 jit_solution(18071585750592534816)
XLA Ops:
  0.0 0.8 %fusion.37 = (f32[16,1024]{1,0:T(8,128)S(1)}, bf16[16,1024]{1,0:T(8,128)(2,1)S(1)}) fusion(s32[1024]{0:T(1024)} %param.11), kind=kLoop, calls=%fused_computation.71 | loop fusion | flops 49152 | bytes 102400 | tf_op jit(solution)/shard_map/convert_element_type | solution.py:89
  0.9 0.8 copy-done
  1.6 1.2 %fusion.29 = bf16[16,2,1024]{2,0,1:T(8,128)(2,1)S(1)} fusion(bf16[1024,1024]{1,0:T(8,128)(2,1)S(1)} %copy-done, bf16[16,1024]{1,0:T(8,128)(2,1)S(1)} %get-tuple-element.91, bf16[2,1024]{1,0:T(2,128)(2,1)} %param.10), kind=kOutput, calls=%fused_computation.61 | convolution fusion | flops 67174400 | bytes 2199552 | tf_op jit(solution)/shard_map/rbp,pk->brk/dot_general | solution.py:70
  2.8 0.4 copy.42
  3.2 1.2 %reshape.173 = bf16[8,2,2048]{2,1,0:T(2,128)(2,1)} reshape(bf16[1024,2,16]{2,1,0:T(2,128)(2,1)S(1)} %bitcast.51) | data formatting | bytes 131072
  4.4 7.3 %all-to-all-start = ((bf16[8,2,2048]{2,1,0:T(2,128)(2,1)}), bf16[8,2,2048]{2,1,0:T(2,128)(2,1)S(1)}, u32[]{:S(2)}, u32[]{:S(2)}) async-start(bf16[8,2,2048]{2,1,0:T(2,128)(2,1)} %reshape.173), calls=%async_computation | async-start | bytes 131072 | tf_op jit(solution)/shard_map/all_to_all | solution.py:73
  11.7 0.1 fusion.33
  11.8 6.8 %all-to-all-done = bf16[8,2,2048]{2,1,0:T(2,128)(2,1)S(1)} async-done(((bf16[8,2,2048]{2,1,0:T(2,128)(2,1)}), bf16[8,2,2048]{2,1,0:T(2,128)(2,1)S(1)}, u32[]{:S(2)}, u32[]{:S(2)}) %all-to-all-start) | async-done | bytes 65568 | tf_op jit(solution)/shard_map/all_to_all | solution.py:73
  18.6 0.4 reshape.174
  19.0 0.3 copy.43
  19.3 5.8 %all_gather.3 = bf16[128,8,128]{2,0,1:T(8,128)(2,1)S(1)} all-gather(bf16[128,2,128]{2,0,1:T(8,128)(2,1)S(1)} %bitcast.53), channel_id=1, replica_groups=mesh['dom'=8,'tm'=4] {'tm'}, dimensions={1}, use_global_device_ids=true | all-gather | bytes 327680 | tf_op jit(solution)/shard_map/all_gather | solution.py:76
  25.1 39.9 %conditional.1 = (bf16[128,2,128]{2,0,1:T(8,128)(2,1)S(1)}) conditional(s32[]{:T(128)} %convert_element_type.158, () %tuple.13, (s32[]{:T(128)}, s32[128,8]{0,1:T(8,128)S(1)}, bf16[64,8,128]{2,1,0:T(8,128)(2,1)S(1)}, bf16[128,8]{1,0:T(8,128)(2,1)S(1)}, s32[128,8]{0,1:T(8,128)S(1)}, /*index=5*/bf16[128,8,128]{2,0,1:T(8,128)(2,1)S(1)}) %tuple.27), branch_computations={%region_0.0_spmd, %region_1.3_spmd} | conditional | flops 13881379 | bytes 45001176 | solution.py:84
  25.1 0.1 copy.45
  25.2 0.1 reshape.154
  25.3 0.1 copy.44
  25.4 0.1 reshape.151
  25.6 5.3 %gather_fusion = bf16[1024,1024]{1,0:T(8,128)(2,1)} fusion(bf16[64,1024]{1,0:T(8,128)(2,1)S(1)} %bitcast.48, s32[1024]{0:T(1024)S(1)} %broadcast_clamp_fusion.1), kind=kCustom, calls=%fused_computation | custom fusion | bytes 4198400 | tf_op jit(solution)/shard_map/cond/branch_1_fun/while/body/eval_jaxpr/jit(_take)/gather | solution.py:59
  30.9 3.9 %copy.38 = bf16[1024,1024]{0,1:T(8,128)(2,1)} copy(bf16[1024,1024]{1,0:T(8,128)(2,1)} %gather_fusion) | data formatting | bytes 4194304 | tf_op jit(solution)/shard_map/cond/branch_1_fun/while/body/eval_jaxpr/jit(_take)/gather | solution.py:59
  34.8 3.9 %copy.39 = bf16[1024,8,128]{2,0,1:T(8,128)(2,1)} copy(bf16[1024,8,128]{0,2,1:T(8,128)(2,1)} %bitcast.49) | data formatting | bytes 4194304 | tf_op jit(solution)/shard_map/cond/branch_1_fun/while/body/eval_jaxpr/jit(_take)/gather | solution.py:59
  38.7 0.1 reshape.152
  38.8 0.1 reshape.149
  38.9 0.1 mul.98
  39.0 3.3 %select_multiply_fusion = bf16[1024,8,128]{2,0,1:T(8,128)(2,1)} fusion(bf16[1024,8,128]{2,0,1:T(8,128)(2,1)} %copy.39, pred[1024]{0:T(1024)(128)(4,1)S(1)} %get-tuple-element.89, bf16[1024]{0:T(1024)(128)(2,1)S(1)} %mul.98), kind=kLoop, calls=%fused_computation.2 | loop fusion | flops 2097152 | bytes 4197376 | tf_op jit(solution)/shard_map/cond/branch_1_fun/while/body/eval_jaxpr/mul | solution.py:59
  42.4 5.4 %gather_fusion.1 = bf16[1024,1024]{1,0:T(8,128)(2,1)} fusion(bf16[128,1024]{1,0:T(8,128)(2,1)S(1)} %copy_bitcast_fusion, s32[1024]{0:T(1024)S(1)} %broadcast_clamp_fusion), kind=kCustom, calls=%fused_computation.1 | custom fusion | bytes 4198400 | tf_op jit(solution)/shard_map/cond/branch_1_fun/while/body/eval_jaxpr/jit(_take)/gather | solution.py:62
  47.7 3.9 %copy.40 = bf16[1024,1024]{0,1:T(8,128)(2,1)} copy(bf16[1024,1024]{1,0:T(8,128)(2,1)} %gather_fusion.1) | data formatting | bytes 4194304 | tf_op jit(solution)/shard_map/cond/branch_1_fun/while/body/eval_jaxpr/jit(_take)/gather | solution.py:62
  51.7 3.9 %copy.41 = bf16[1024,8,128]{2,0,1:T(8,128)(2,1)} copy(bf16[1024,8,128]{0,2,1:T(8,128)(2,1)} %bitcast.50) | data formatting | bytes 4194304 | tf_op jit(solution)/shard_map/cond/branch_1_fun/while/body/eval_jaxpr/jit(_take)/gather | solution.py:62
  55.6 3.2 %broadcast_select_fusion = bf16[1024,8,128]{2,0,1:T(8,128)(2,1)} fusion(bf16[1024,8,128]{2,0,1:T(8,128)(2,1)} %copy.41, pred[1024]{0:T(1024)(128)(4,1)S(1)} %get-tuple-element.88), kind=kLoop, calls=%fused_computation.3 | loop fusion | flops 1048576 | bytes 4195328 | tf_op jit(solution)/shard_map/cond/branch_1_fun/while/body/eval_jaxpr/jit(_take)/select_n | solution.py:62
  58.7 3.0 %fusion.15 = f32[128,8,1,128]{3,1,0,2:T(8,128)S(1)} fusion(bf16[1024,8,128]{2,0,1:T(8,128)(2,1)} %select_multiply_fusion, s32[]{:T(128)S(6)} %min.50, pred[]{:T(512)S(6)} %ge.70, pred[]{:T(512)S(6)} %ge.68, pred[]{:T(512)S(6)} %ge.67, pred[]{:T(512)S(6)} %ge.66, pred[]{:T(512)S(6)} %ge.65, pred[]{:T(512)S(6)} %ge.64, pred[]{:T(512)S(6)} %ge.63, pred[]{:T(512)S(6)} %ge.60, ...), kind=kLoop, calls=%fused_computation.36 | loop fusion | flops 5111808 | bytes 4718632 | tf_op jit(solution)/shard_map/cond/branch_1_fun/while/body/eval_jaxpr/stack | solution.py:26
  61.7 3.0 %fusion.7 = f32[128,8,1,128]{3,1,0,2:T(8,128)S(1)} fusion(bf16[1024,8,128]{2,0,1:T(8,128)(2,1)} %select_multiply_fusion, s32[]{:T(128)S(6)} %min.49, pred[]{:T(512)S(6)} %ge.69, pred[]{:T(512)S(6)} %ge.68, pred[]{:T(512)S(6)} %ge.67, pred[]{:T(512)S(6)} %ge.66, pred[]{:T(512)S(6)} %ge.65, pred[]{:T(512)S(6)} %ge.64, pred[]{:T(512)S(6)} %ge.63, pred[]{:T(512)S(6)} %ge.60, ...), kind=kLoop, calls=%fused_computation.28 | loop fusion | flops 5111808 | bytes 4718632 | tf_op jit(solution)/shard_map/cond/branch_1_fun/while/body/eval_jaxpr/stack | solution.py:26
  64.8 0.3 maximum_reduce_fusion
  65.1 9.3 %all_to_all.36 = bf16[128,2,128]{2,1,0:T(2,128)(2,1)S(1)} all-to-all(bf16[128,2,128]{2,1,0:T(2,128)(2,1)S(1)} %copy.55), channel_id=1, replica_groups=mesh['dom'=8,'tm'=4] {'dom'}, dimensions={0} | all-to-all | bytes 131072 | tf_op jit(solution)/shard_map/all_to_all | solution.py:85
  74.5 2.9 %fusion.26 = bf16[2,1024]{1,0:T(2,128)(2,1)} fusion(bf16[16,2,1024]{2,0,1:T(8,128)(2,1)S(1)} %all_to_all.33, bf16[1024,1024]{1,0:T(8,128)(2,1)} %param.13, f32[16,1024]{1,0:T(8,128)S(1)} %get-tuple-element.90), kind=kOutput, calls=%fused_computation.60 | convolution fusion | flops 67172352 | bytes 2232320 | tf_op jit(solution)/shard_map/brk,pk->brp/dot_general | solution.py:88
  (18 shorter events, 0.2 us)
Async XLA Ops:
  0.0 1.6 %copy-start = (bf16[1024,1024]{1,0:T(8,128)(2,1)S(1)}, bf16[1024,1024]{1,0:T(8,128)(2,1)}, u32[]{:S(2)}) copy-start(bf16[1024,1024]{1,0:T(8,128)(2,1)} %param.12) | copy-start | bytes 6291460
  0.0 11.7 %copy-start.4 = (s32[128]{0:T(128)S(1)}, s32[128]{0:T(128)}, u32[]{:S(2)}) copy-start(s32[128]{0:T(128)} %param.17) | copy-start | bytes 1540
  1.6 23.5 %copy-start.1 = (bf16[64,8,128]{2,1,0:T(8,128)(2,1)S(1)}, bf16[64,8,128]{2,1,0:T(8,128)(2,1)}, u32[]{:S(2)}) copy-start(bf16[64,8,128]{2,1,0:T(8,128)(2,1)} %param.14) | copy-start | bytes 393220
  1.6 23.5 %copy-start.2 = (s32[128,8]{0,1:T(8,128)S(1)}, s32[128,8]{0,1:T(8,128)}, u32[]{:S(2)}) copy-start(s32[128,8]{0,1:T(8,128)} %param.16) | copy-start | bytes 12292
  1.6 23.5 %copy-start.3 = (s32[128,8]{0,1:T(8,128)S(1)}, s32[128,8]{0,1:T(8,128)}, u32[]{:S(2)}) copy-start(s32[128,8]{0,1:T(8,128)} %param.15) | copy-start | bytes 12292
  4.4 14.2 %all-to-all-start = ((bf16[8,2,2048]{2,1,0:T(2,128)(2,1)}), bf16[8,2,2048]{2,1,0:T(2,128)(2,1)S(1)}, u32[]{:S(2)}, u32[]{:S(2)}) async-start(bf16[8,2,2048]{2,1,0:T(2,128)(2,1)} %reshape.173), calls=%async_computation | async-start | bytes 131072 | tf_op jit(solution)/shard_map/all_to_all | solution.py:73
where the time goes:
time: 78 us; the launch traced here: 77.4 us
  local copies, waits for them, and re-layouts  30.3 us (39%)
  blocking collectives  15.1 us (19%)
  other arithmetic  13.7 us (18%)
  starting transfers between devices  7.31 us (9%)
  waiting for transfers between devices  6.81 us (9%)
  matrix products  4.12 us (5%)
    gather x3, local copies, waits for them, and re-layouts, one_block(): jnp.take(flat_rays, sources, axis=0)  13.2 us
    gather x3, local copies, waits for them, and re-layouts, one_block(): jnp.take(flat_table, classes, axis=0) * keep_rows  13.2 us
    all_to_all x1, blocking collectives, body(): lax.all_to_all(incoming.astype(jnp.bfloat16), 'dom', split_axis=0, concat...  9.29 us
    all_to_all x1, starting transfers between devices, body(): lax.all_to_all(outgoing, 'dom', split_axis=2, concat_axis=0, tiled=True)  7.31 us
    all_to_all x1, waiting for transfers between devices, body(): lax.all_to_all(outgoing, 'dom', split_axis=2, concat_axis=0, tiled=True)  6.81 us
    another operation x2, other arithmetic, lag_sum(): return jnp.stack(results, axis=1)  6.01 us
    all_gather x1, blocking collectives, body(): piece = lax.all_gather(spread, 'tm', axis=1, tiled=True)  5.78 us
    mul x1, other arithmetic, one_block(): jnp.take(flat_table, classes, axis=0) * keep_rows  3.27 us
  transfers between devices with their start and end apart: 1, of which 1 were waited for; matrix products, arithmetic and copies ran while one was open for 0% of the time, Pallas kernels for 0%

commit v1 on v0

--- a/solution.py
+++ b/solution.py
@@ -82,8 +82,14 @@
         return empty
 
     incoming = lax.cond(jnp.int32(0) <= first + rows_own - 1, active, passive)
-    rays = lax.all_to_all(
-        incoming.astype(jnp.bfloat16), "dom", split_axis=0, concat_axis=2, tiled=True
+    rays = jnp.concatenate(
+        lax.all_to_all(
+            jnp.stack(jnp.split(incoming.astype(jnp.bfloat16), lax.axis_size("dom"), axis=0)),
+            "dom",
+            0,
+            0,
+        ),
+        axis=2,
     )
     partial_value = jnp.einsum("brk,pk->brp", rays, reception, preferred_element_type=jnp.float32)
     field = jnp.sum(partial_value * box_onehot.astype(jnp.float32)[:, None, :], axis=0)

time: 78 us -> 78 us (level)
    unnamed x12 -> x19, local copies, waits for them, and re-layouts: 2.32 us -> 2.37 us
where the time goes in v1:
time: 78 us; the launch traced here: 77.3 us
  local copies, waits for them, and re-layouts  30.2 us (39%)
  blocking collectives  15.1 us (19%)
  other arithmetic  13.7 us (18%)
  starting transfers between devices  7.31 us (9%)
  waiting for transfers between devices  6.81 us (9%)
  matrix products  4.12 us (5%)
    gather x3, local copies, waits for them, and re-layouts, one_block(): jnp.take(flat_rays, sources, axis=0)  13.2 us
    gather x3, local copies, waits for them, and re-layouts, one_block(): jnp.take(flat_table, classes, axis=0) * keep_rows  13.1 us
    all_to_all x1, blocking collectives, body(): lax.all_to_all(jnp.stack(jnp.split(incoming.astype(jnp.bfloat16), lax.axi...  9.29 us
    all_to_all x1, starting transfers between devices, body(): lax.all_to_all(outgoing, 'dom', split_axis=2, concat_axis=0, tiled=True)  7.31 us
    all_to_all x1, waiting for transfers between devices, body(): lax.all_to_all(outgoing, 'dom', split_axis=2, concat_axis=0, tiled=True)  6.81 us
    another operation x2, other arithmetic, lag_sum(): return jnp.stack(results, axis=1)  6.05 us
    all_gather x1, blocking collectives, body(): piece = lax.all_gather(spread, 'tm', axis=1, tiled=True)  5.78 us
    mul x1, other arithmetic, one_block(): jnp.take(flat_table, classes, axis=0) * keep_rows  3.26 us
  transfers between devices with their start and end apart: 1, of which 1 were waited for; matrix products, arithmetic and copies ran while one was open for 0% of the time, Pallas kernels for 0%

profile of v1, /device:TPU:0, one launch (start us, length us, event | category | flops | bytes accessed | tf_op | source)
XLA Modules:
  0.0 77.3 jit_solution(4245781367347944511)
XLA Ops:
  0.0 0.8 %fusion.39 = (f32[16,1024]{1,0:T(8,128)S(1)}, bf16[16,1024]{1,0:T(8,128)(2,1)S(1)}) fusion(s32[1024]{0:T(1024)} %param.11), kind=kLoop, calls=%fused_computation.87 | loop fusion | flops 49152 | bytes 102400 | tf_op jit(solution)/shard_map/convert_element_type | solution.py:95
  0.9 0.8 copy-done
  1.6 1.2 %fusion.29 = bf16[16,2,1024]{2,0,1:T(8,128)(2,1)S(1)} fusion(bf16[1024,1024]{1,0:T(8,128)(2,1)S(1)} %copy-done, bf16[16,1024]{1,0:T(8,128)(2,1)S(1)} %get-tuple-element.146, bf16[2,1024]{1,0:T(2,128)(2,1)} %param.10), kind=kOutput, calls=%fused_computation.69 | convolution fusion | flops 67174400 | bytes 2199552 | tf_op jit(solution)/shard_map/rbp,pk->brk/dot_general | solution.py:70
  2.8 0.4 copy.34
  3.2 1.2 %reshape.192 = bf16[8,2,2048]{2,1,0:T(2,128)(2,1)} reshape(bf16[1024,2,16]{2,1,0:T(2,128)(2,1)S(1)} %bitcast.66) | data formatting | bytes 131072
  4.4 7.3 %all-to-all-start = ((bf16[8,2,2048]{2,1,0:T(2,128)(2,1)}), bf16[8,2,2048]{2,1,0:T(2,128)(2,1)S(1)}, u32[]{:S(2)}, u32[]{:S(2)}) async-start(bf16[8,2,2048]{2,1,0:T(2,128)(2,1)} %reshape.192), calls=%async_computation | async-start | bytes 131072 | tf_op jit(solution)/shard_map/all_to_all | solution.py:73
  11.7 0.1 fusion.35
  11.8 6.8 %all-to-all-done = bf16[8,2,2048]{2,1,0:T(2,128)(2,1)S(1)} async-done(((bf16[8,2,2048]{2,1,0:T(2,128)(2,1)}), bf16[8,2,2048]{2,1,0:T(2,128)(2,1)S(1)}, u32[]{:S(2)}, u32[]{:S(2)}) %all-to-all-start) | async-done | bytes 65568 | tf_op jit(solution)/shard_map/all_to_all | solution.py:73
  18.6 0.4 reshape.193
  19.0 0.3 copy.35
  19.3 5.8 %all_gather.3 = bf16[128,8,128]{2,0,1:T(8,128)(2,1)S(1)} all-gather(bf16[128,2,128]{2,0,1:T(8,128)(2,1)S(1)} %bitcast.68), channel_id=1, replica_groups=mesh['dom'=8,'tm'=4] {'tm'}, dimensions={1}, use_global_device_ids=true | all-gather | bytes 327680 | tf_op jit(solution)/shard_map/all_gather | solution.py:76
  25.1 39.9 %conditional.1 = (bf16[1,16,2,128]{3,1,2,0:T(8,128)(2,1)S(1)}, bf16[1,16,2,128]{3,1,2,0:T(8,128)(2,1)S(1)}, bf16[1,16,2,128]{3,1,2,0:T(8,128)(2,1)S(1)}, bf16[1,...) conditional(s32[]{:T(128)} %convert_element_type.188, () %tuple.21, ...), branch_computations={%region_0.0_spmd, %region_1.3_spmd} | conditional | flops 13881379 | bytes 45132304 | solution.py:84
  25.1 0.1 copy.37
  25.2 0.1 reshape.169
  25.3 0.1 copy.36
  25.4 0.1 reshape.166
  25.5 5.3 %gather_fusion = bf16[1024,1024]{1,0:T(8,128)(2,1)} fusion(bf16[64,1024]{1,0:T(8,128)(2,1)S(1)} %bitcast.63, s32[1024]{0:T(1024)S(1)} %broadcast_clamp_fusion.1), kind=kCustom, calls=%fused_computation | custom fusion | bytes 4198400 | tf_op jit(solution)/shard_map/cond/branch_1_fun/while/body/eval_jaxpr/jit(_take)/gather | solution.py:59
  30.9 3.9 %copy.30 = bf16[1024,1024]{0,1:T(8,128)(2,1)} copy(bf16[1024,1024]{1,0:T(8,128)(2,1)} %gather_fusion) | data formatting | bytes 4194304 | tf_op jit(solution)/shard_map/cond/branch_1_fun/while/body/eval_jaxpr/jit(_take)/gather | solution.py:59
  34.8 3.9 %copy.31 = bf16[1024,8,128]{2,0,1:T(8,128)(2,1)} copy(bf16[1024,8,128]{0,2,1:T(8,128)(2,1)} %bitcast.64) | data formatting | bytes 4194304 | tf_op jit(solution)/shard_map/cond/branch_1_fun/while/body/eval_jaxpr/jit(_take)/gather | solution.py:59
  38.7 0.1 reshape.167
  38.8 0.1 reshape.164
  38.9 0.1 mul.115
  39.0 3.3 %select_multiply_fusion = bf16[1024,8,128]{2,0,1:T(8,128)(2,1)} fusion(bf16[1024,8,128]{2,0,1:T(8,128)(2,1)} %copy.31, pred[1024]{0:T(1024)(128)(4,1)S(1)} %get-tuple-element.144, bf16[1024]{0:T(1024)(128)(2,1)S(1)} %mul.115), kind=kLoop, calls=%fused_computation.2 | loop fusion | flops 2097152 | bytes 4197376 | tf_op jit(solution)/shard_map/cond/branch_1_fun/while/body/eval_jaxpr/mul | solution.py:59
  42.3 5.4 %gather_fusion.1 = bf16[1024,1024]{1,0:T(8,128)(2,1)} fusion(bf16[128,1024]{1,0:T(8,128)(2,1)S(1)} %copy_bitcast_fusion, s32[1024]{0:T(1024)S(1)} %broadcast_clamp_fusion), kind=kCustom, calls=%fused_computation.1 | custom fusion | bytes 4198400 | tf_op jit(solution)/shard_map/cond/branch_1_fun/while/body/eval_jaxpr/jit(_take)/gather | solution.py:62
  47.7 3.9 %copy.32 = bf16[1024,1024]{0,1:T(8,128)(2,1)} copy(bf16[1024,1024]{1,0:T(8,128)(2,1)} %gather_fusion.1) | data formatting | bytes 4194304 | tf_op jit(solution)/shard_map/cond/branch_1_fun/while/body/eval_jaxpr/jit(_take)/gather | solution.py:62
  51.6 3.9 %copy.33 = bf16[1024,8,128]{2,0,1:T(8,128)(2,1)} copy(bf16[1024,8,128]{0,2,1:T(8,128)(2,1)} %bitcast.65) | data formatting | bytes 4194304 | tf_op jit(solution)/shard_map/cond/branch_1_fun/while/body/eval_jaxpr/jit(_take)/gather | solution.py:62
  55.5 3.2 %broadcast_select_fusion = bf16[1024,8,128]{2,0,1:T(8,128)(2,1)} fusion(bf16[1024,8,128]{2,0,1:T(8,128)(2,1)} %copy.33, pred[1024]{0:T(1024)(128)(4,1)S(1)} %get-tuple-element.143), kind=kLoop, calls=%fused_computation.3 | loop fusion | flops 1048576 | bytes 4195328 | tf_op jit(solution)/shard_map/cond/branch_1_fun/while/body/eval_jaxpr/jit(_take)/select_n | solution.py:62
  58.7 3.0 %fusion.15 = f32[128,8,1,128]{3,1,0,2:T(8,128)S(1)} fusion(bf16[1024,8,128]{2,0,1:T(8,128)(2,1)} %select_multiply_fusion, s32[]{:T(128)S(6)} %min.66, pred[]{:T(512)S(6)} %ge.88, pred[]{:T(512)S(6)} %ge.86, pred[]{:T(512)S(6)} %ge.85, pred[]{:T(512)S(6)} %ge.84, pred[]{:T(512)S(6)} %ge.83, pred[]{:T(512)S(6)} %ge.82, pred[]{:T(512)S(6)} %ge.81, pred[]{:T(512)S(6)} %ge.78, ...), kind=kLoop, calls=%fused_computation.36 | loop fusion | flops 5111808 | bytes 4718632 | tf_op jit(solution)/shard_map/cond/branch_1_fun/while/body/eval_jaxpr/stack | solution.py:26
  61.6 3.1 %fusion.7 = f32[128,8,1,128]{3,1,0,2:T(8,128)S(1)} fusion(bf16[1024,8,128]{2,0,1:T(8,128)(2,1)} %select_multiply_fusion, s32[]{:T(128)S(6)} %min.65, pred[]{:T(512)S(6)} %ge.87, pred[]{:T(512)S(6)} %ge.86, pred[]{:T(512)S(6)} %ge.85, pred[]{:T(512)S(6)} %ge.84, pred[]{:T(512)S(6)} %ge.83, pred[]{:T(512)S(6)} %ge.82, pred[]{:T(512)S(6)} %ge.81, pred[]{:T(512)S(6)} %ge.78, ...), kind=kLoop, calls=%fused_computation.28 | loop fusion | flops 5111808 | bytes 4718632 | tf_op jit(solution)/shard_map/cond/branch_1_fun/while/body/eval_jaxpr/stack | solution.py:26
  64.7 0.3 maximum_reduce_fusion
  65.1 9.3 %all_to_all.23 = bf16[8,16,2,128]{3,1,2,0:T(8,128)(2,1)S(1)} all-to-all(bf16[8,16,2,128]{3,1,2,0:T(8,128)(2,1)S(1)} %constant_dynamic-update-slice_fusion), channel_id=1, replica_groups=mesh['dom'=8,'tm'=4] {'dom'}, dimensions={0} | all-to-all | bytes 131072 | tf_op jit(solution)/shard_map/all_to_all | solution.py:86
  74.4 2.9 %fusion.26 = bf16[2,1024]{1,0:T(2,128)(2,1)} fusion(bf16[1024,1024]{1,0:T(8,128)(2,1)} %param.13, f32[16,1024]{1,0:T(8,128)S(1)} %get-tuple-element.145, bf16[8,16,2,128]{3,1,2,0:T(8,128)(2,1)S(1)} %all_to_all.23), kind=kOutput, calls=%fused_computation.68 | convolution fusion | flops 67172352 | bytes 2232320 | tf_op jit(solution)/shard_map/brk,pk->brp/dot_general | solution.py:94
  (24 shorter events, 0.2 us)
Async XLA Ops:
  0.0 1.6 %copy-start = (bf16[1024,1024]{1,0:T(8,128)(2,1)S(1)}, bf16[1024,1024]{1,0:T(8,128)(2,1)}, u32[]{:S(2)}) copy-start(bf16[1024,1024]{1,0:T(8,128)(2,1)} %param.12) | copy-start | bytes 6291460
  0.0 11.7 %copy-start.4 = (s32[128]{0:T(128)S(1)}, s32[128]{0:T(128)}, u32[]{:S(2)}) copy-start(s32[128]{0:T(128)} %param.17) | copy-start | bytes 1540
  1.6 23.5 %copy-start.1 = (bf16[64,8,128]{2,1,0:T(8,128)(2,1)S(1)}, bf16[64,8,128]{2,1,0:T(8,128)(2,1)}, u32[]{:S(2)}) copy-start(bf16[64,8,128]{2,1,0:T(8,128)(2,1)} %param.14) | copy-start | bytes 393220
  1.6 23.5 %copy-start.2 = (s32[128,8]{0,1:T(8,128)S(1)}, s32[128,8]{0,1:T(8,128)}, u32[]{:S(2)}) copy-start(s32[128,8]{0,1:T(8,128)} %param.16) | copy-start | bytes 12292
  1.6 23.5 %copy-start.3 = (s32[128,8]{0,1:T(8,128)S(1)}, s32[128,8]{0,1:T(8,128)}, u32[]{:S(2)}) copy-start(s32[128,8]{0,1:T(8,128)} %param.15) | copy-start | bytes 12292
  4.4 14.2 %all-to-all-start = ((bf16[8,2,2048]{2,1,0:T(2,128)(2,1)}), bf16[8,2,2048]{2,1,0:T(2,128)(2,1)S(1)}, u32[]{:S(2)}, u32[]{:S(2)}) async-start(bf16[8,2,2048]{2,1,0:T(2,128)(2,1)} %reshape.192), calls=%async_computation | async-start | bytes 131072 | tf_op jit(solution)/shard_map/all_to_all | solution.py:73
